TPU v7x, 32 devices: a whole 2x2x4 slice. The times are simulated.
32 devices in a mesh: grp: 2 (over y), dev: 16 (over z, x, core).
Axes of the slice: x: 2, y: 2, z: 4, core: 2. Of those that a mesh axis runs over, the one named last changes fastest.
Arguments:
- sources: bfloat16 [65536, 768], P(('grp', 'dev')), may hold values from -6 to 6
- encoder: bfloat16 [65536, 256], P(('grp', 'dev')), may hold values from -0.125 to 0.125
- section_weight: bfloat16 [32, 4, 2, 256, 256], P(('grp', 'dev')), may hold values from -0.25 to 0.25
- cross_weight: bfloat16 [2, 16, 2, 256, 256], P('grp', 'dev'), may hold values from -0.25 to 0.25
- local_weight: bfloat16 [32, 14, 256, 256], P(('grp', 'dev')), may hold values from -0.375 to 0.375
- decoder: bfloat16 [65536, 256], P(('grp', 'dev')), may hold values from -0.375 to 0.375
Outputs:
- target_values: bfloat16 [65536, 768], P(('grp', 'dev'))
All inputs are finite; a program needn't handle non-finite values.
Results may differ from a plain program's by a relative error of at most 0.02.
Values may be sent and summed in bfloat16 or wider, within the bound.
No kernel may reach another device: no remote copies, remote signals or barrier semaphores. Data moves between devices by JAX's collectives and lax.ppermute only.
A program may use at most 64 MiB of HBM per device.

v0:
```python
import jax
import jax.numpy as jnp
from jax import lax
from jax.sharding import PartitionSpec as P

K = 256
LOCAL = 3


def from_partner(block, axis, bit):
    count = lax.axis_size(axis)
    route = []
    for low in range(count):
        high = low | 1 << bit
        if high != low and high < count:
            route += [(low, high), (high, low)]
    return lax.ppermute(block, axis, route)


def shards(sources, encoder, section_weight, cross_weight, local_weight, decoder):
    coeffs = lax.dot_general(
        encoder, sources, (((0,), (0,)), ((), ())), preferred_element_type=jnp.float32
    ).astype(jnp.bfloat16)
    section_count = lax.axis_size("dev").bit_length() - 1
    for section_bit in range(section_count):
        partner = from_partner(coeffs, "dev", section_bit)
        keep_matrix = section_weight[0, section_bit, 0]
        take_matrix = section_weight[0, section_bit, 1]
        coeffs = (
            jnp.dot(keep_matrix, coeffs, preferred_element_type=jnp.float32)
            + jnp.dot(take_matrix, partner, preferred_element_type=jnp.float32)
        ).astype(jnp.bfloat16)
    own_cross = cross_weight[0, 0]
    merged = jnp.einsum(
        "hkl,hlr->kr",
        own_cross,
        lax.all_gather(coeffs[None], "grp", axis=0, tiled=True),
        preferred_element_type=jnp.float32,
    ).astype(jnp.bfloat16)
    blocks = merged[None]
    offset = 0
    for depth_level in range(LOCAL):
        children = 2 ** (depth_level + 1)
        matrices = local_weight[0, offset : offset + children].reshape(children // 2, 2, K, K)
        blocks = jnp.einsum("jckl,jlr->jckr", matrices, blocks, preferred_element_type=jnp.float32)
        blocks = blocks.reshape(children, K, blocks.shape[-1]).astype(jnp.bfloat16)
        offset = offset + children
    decoder_leaves = decoder.reshape(2**LOCAL, -1, K)
    target_values = jnp.einsum(
        "ctk,ckr->ctr", decoder_leaves, blocks, preferred_element_type=jnp.float32
    )
    return target_values.reshape(-1, blocks.shape[-1]).astype(jnp.bfloat16)


def solution(mesh):
    placed = (
        P(("grp", "dev"), None),
        P(("grp", "dev"), None),
        P(("grp", "dev"), None, None, None, None),
        P("grp", "dev", None, None, None),
        P(("grp", "dev"), None, None, None),
        P(("grp", "dev"), None),
    )
    return jax.shard_map(
        shards, mesh=mesh, in_specs=placed, out_specs=P(("grp", "dev"), None), check_vma=False
    )
```

profile of v0, /device:TPU:0, one launch (start us, length us, event | category | flops | bytes accessed | tf_op | source)
XLA Modules:
  0.0 69.3 jit_solution(10886615628694809823)
XLA Ops:
  0.0 0.0 copy-start
  0.0 0.0 copy-start.3
  0.0 1.9 %copy-done = bf16[2048,768]{1,0:T(8,128)(2,1)S(1)} copy-done((bf16[2048,768]{1,0:T(8,128)(2,1)S(1)}, bf16[2048,768]{1,0:T(8,128)(2,1)}, u32[]{:S(2)}) %copy-start) | copy-done | bytes 3145752
  1.9 2.2 %convolution_convert_fusion.4 = bf16[256,768]{1,0:T(8,128)(2,1)S(1)} fusion(bf16[2048,256]{1,0:T(8,128)(2,1)} %param.7, bf16[2048,768]{1,0:T(8,128)(2,1)S(1)} %copy-done), kind=kOutput, calls=%fused_computation.15 | convolution fusion | flops 805502976 | bytes 4587520 | tf_op jit(solution)/shard_map/dot_general | solution.py:21
  4.1 0.6 collective-permute-start
  4.7 0.0 copy-done.3
  4.7 0.3 fusion.25
  5.0 1.0 %collective-permute-done = bf16[256,768]{1,0:T(8,128)(2,1)S(1)} collective-permute-done((bf16[256,768]{1,0:T(8,128)(2,1)S(1)}, bf16[256,768]{1,0:T(8,128)(2,1)S(1)}, u32[]{:S(2)}, u32[]{:S(2)}) %collective-permute-start) | collective-permute-done | bytes 393248 | tf_op jit(solution)/shard_map/ppermute | solution.py:17
  6.0 0.3 fusion.1
  6.4 0.0 copy-start.1
  6.4 2.9 %collective-permute-start.1 = (bf16[256,768]{0,1:T(8,128)(2,1)S(1)}, bf16[256,768]{0,1:T(8,128)(2,1)S(1)}, u32[]{:S(2)}, u32[]{:S(2)}) collective-permute-start(bf16[256,768]{0,1:T(8,128)(2,1)S(1)} %bitcast.93), channel_id=1, source_target_pairs={{0,2},{2,0},{1,3},{3,1},{4,6},{6,4},{5,7},{7,5},{8,10},{10,8},{9,1... | collective-permute-start | bytes 1179656 | tf_op jit(solution)/shard_map/ppermute | solution.py:17
  9.3 0.3 fusion.22
  9.6 9.1 %collective-permute-done.1 = bf16[256,768]{0,1:T(8,128)(2,1)S(1)} collective-permute-done((bf16[256,768]{0,1:T(8,128)(2,1)S(1)}, bf16[256,768]{0,1:T(8,128)(2,1)S(1)}, u32[]{:S(2)}, u32[]{:S(2)}) %collective-permute-start.1) | collective-permute-done | bytes 393248 | tf_op jit(solution)/shard_map/ppermute | solution.py:17
  18.7 0.3 fusion.2
  19.0 1.9 %collective-permute-start.2 = (bf16[256,768]{0,1:T(8,128)(2,1)S(1)}, bf16[256,768]{0,1:T(8,128)(2,1)S(1)}, u32[]{:S(2)}, u32[]{:S(2)}) collective-permute-start(bf16[256,768]{0,1:T(8,128)(2,1)S(1)} %bitcast.94), channel_id=1, source_target_pairs={{0,4},{4,0},{1,5},{5,1},{2,6},{6,2},{3,7},{7,3},{8,12},{12,8},{9,1... | collective-permute-start | bytes 1179656 | tf_op jit(solution)/shard_map/ppermute | solution.py:17
  20.9 0.3 fusion.19
  21.2 8.5 %collective-permute-done.2 = bf16[256,768]{0,1:T(8,128)(2,1)S(1)} collective-permute-done((bf16[256,768]{0,1:T(8,128)(2,1)S(1)}, bf16[256,768]{0,1:T(8,128)(2,1)S(1)}, u32[]{:S(2)}, u32[]{:S(2)}) %collective-permute-start.2) | collective-permute-done | bytes 393248 | tf_op jit(solution)/shard_map/ppermute | solution.py:17
  29.6 0.3 fusion.3
  29.9 2.6 %collective-permute-start.3 = (bf16[256,768]{0,1:T(8,128)(2,1)S(1)}, bf16[256,768]{0,1:T(8,128)(2,1)S(1)}, u32[]{:S(2)}, u32[]{:S(2)}) collective-permute-start(bf16[256,768]{0,1:T(8,128)(2,1)S(1)} %bitcast.92), channel_id=1, source_target_pairs={{0,8},{8,0},{1,9},{9,1},{2,10},{10,2},{3,11},{11,3},{4,12},{12,4},... | collective-permute-start | bytes 1179656 | tf_op jit(solution)/shard_map/ppermute | solution.py:17
  32.6 0.0 copy-done.1
  32.6 0.8 %slice.42 = bf16[1,4,256,256]{3,2,1,0:T(8,128)(2,1)} slice(bf16[1,14,256,256]{3,2,1,0:T(8,128)(2,1)S(1)} %copy-done.1), slice={[0:1], [2:6], [0:256], [0:256]} | slice | bytes 1048576 | tf_op jit(solution)/shard_map/slice | solution.py:44
  33.4 1.0 %slice.43 = bf16[1,8,256,256]{3,2,1,0:T(8,128)(2,1)} slice(bf16[1,14,256,256]{3,2,1,0:T(8,128)(2,1)S(1)} %copy-done.1), slice={[0:1], [6:14], [0:256], [0:256]} | slice | bytes 2097152 | tf_op jit(solution)/shard_map/slice | solution.py:44
  34.4 0.3 fusion.16
  34.7 14.3 %collective-permute-done.3 = bf16[256,768]{0,1:T(8,128)(2,1)S(1)} collective-permute-done((bf16[256,768]{0,1:T(8,128)(2,1)S(1)}, bf16[256,768]{0,1:T(8,128)(2,1)S(1)}, u32[]{:S(2)}, u32[]{:S(2)}) %collective-permute-start.3) | collective-permute-done | bytes 393248 | tf_op jit(solution)/shard_map/ppermute | solution.py:17
  49.1 0.3 fusion.6
  49.4 11.0 %all-gather = bf16[512,768]{0,1:T(8,128)(2,1)S(1)} all-gather(bf16[256,768]{0,1:T(8,128)(2,1)S(1)} %fusion.6), channel_id=2, replica_groups=mesh['grp'=2,'dev'=16] {'grp'}, dimensions={0}, use_global_device_ids=true | all-gather | bytes 1179648 | tf_op jit(solution)/shard_map/all_gather | solution.py:37
  60.4 0.0 copy-done.4
  60.4 0.4 fusion.7
  60.8 3.1 %convolution_convert_fusion.2 = bf16[2,768,2,256]{3,1,2,0:T(8,128)(2,1)} fusion(bf16[2,2,256,256]{3,2,1,0:T(8,128)(2,1)} %bitcast.91, bf16[768,256,1]{1,0,2:T(8,128)(2,1)S(1)} %fusion.7, bf16[1,14,256,256]{3,2,1,0:T(8,128)(2,1)} %param.10), kind=kOutput, calls=%fused_computation.2 | convolution fusion | flops 605159424 | bytes 2752512 | tf_op jit(solution)/shard_map/jckl,jlr->jckr/dot_general | solution.py:45
  63.8 2.8 %convolution_convert_fusion.1 = bf16[4,768,2,256]{3,1,2,0:T(8,128)(2,1)S(1)} fusion(bf16[4,256,768,1]{1,2,3,0:T(8,128)(2,1)} %bitcast.89, bf16[4,2,256,256]{3,2,1,0:T(8,128)(2,1)} %bitcast.90), kind=kOutput, calls=%fused_computation.1 | convolution fusion | flops 806879232 | bytes 5767168 | tf_op jit(solution)/shard_map/jckl,jlr->jckr/dot_general | solution.py:45
  66.7 0.0 copy-done.2
  66.7 2.7 %convolution_convert_fusion = bf16[8,768,256]{1,2,0:T(8,128)(2,1)} fusion(bf16[8,256,768]{1,2,0:T(8,128)(2,1)S(1)} %bitcast.88, bf16[8,256,256]{2,1,0:T(8,128)(2,1)S(1)} %bitcast.95), kind=kOutput, calls=%fused_computation | convolution fusion | flops 806879232 | bytes 7340032 | tf_op jit(solution)/shard_map/ctk,ckr->ctr/dot_general | solution.py:49
  (2 shorter events, 0.0 us)
Async XLA Ops:
  0.0 1.9 %copy-start = (bf16[2048,768]{1,0:T(8,128)(2,1)S(1)}, bf16[2048,768]{1,0:T(8,128)(2,1)}, u32[]{:S(2)}) copy-start(bf16[2048,768]{1,0:T(8,128)(2,1)} %param.6) | copy-start | bytes 9437188
  0.0 4.7 %copy-start.3 = (bf16[1,4,2,256,256]{4,3,2,1,0:T(8,128)(2,1)S(1)}, bf16[1,4,2,256,256]{4,3,2,1,0:T(8,128)(2,1)}, u32[]{:S(2)}) copy-start(bf16[1,4,2,256,256]{4,3,2,1,0:T(8,128)(2,1)} %param.8) | copy-start | bytes 3145732
  4.1 1.9 %collective-permute-start = (bf16[256,768]{1,0:T(8,128)(2,1)S(1)}, bf16[256,768]{1,0:T(8,128)(2,1)S(1)}, u32[]{:S(2)}, u32[]{:S(2)}) collective-permute-start(bf16[256,768]{1,0:T(8,128)(2,1)S(1)} %convolution_convert_fusion.4), channel_id=1, source_target_pairs={{0,1},{1,0},{2,3},{3,2},{4,5},{5,4},{6,7},{7,6},{8,9},{9,8},{10,11... | collective-permute-start | bytes 1179656 | tf_op jit(solution)/shard_map/ppermute | solution.py:17
  6.4 26.2 %copy-start.1 = (bf16[1,14,256,256]{3,2,1,0:T(8,128)(2,1)S(1)}, bf16[1,14,256,256]{3,2,1,0:T(8,128)(2,1)}, u32[]{:S(2)}) copy-start(bf16[1,14,256,256]{3,2,1,0:T(8,128)(2,1)} %param.10) | copy-start | bytes 5505028
  6.4 12.3 %collective-permute-start.1 = (bf16[256,768]{0,1:T(8,128)(2,1)S(1)}, bf16[256,768]{0,1:T(8,128)(2,1)S(1)}, u32[]{:S(2)}, u32[]{:S(2)}) collective-permute-start(bf16[256,768]{0,1:T(8,128)(2,1)S(1)} %bitcast.93), channel_id=1, source_target_pairs={{0,2},{2,0},{1,3},{3,1},{4,6},{6,4},{5,7},{7,5},{8,10},{10,8},{9,1... | collective-permute-start | bytes 1179656 | tf_op jit(solution)/shard_map/ppermute | solution.py:17
  19.0 10.7 %collective-permute-start.2 = (bf16[256,768]{0,1:T(8,128)(2,1)S(1)}, bf16[256,768]{0,1:T(8,128)(2,1)S(1)}, u32[]{:S(2)}, u32[]{:S(2)}) collective-permute-start(bf16[256,768]{0,1:T(8,128)(2,1)S(1)} %bitcast.94), channel_id=1, source_target_pairs={{0,4},{4,0},{1,5},{5,1},{2,6},{6,2},{3,7},{7,3},{8,12},{12,8},{9,1... | collective-permute-start | bytes 1179656 | tf_op jit(solution)/shard_map/ppermute | solution.py:17
  29.9 19.1 %collective-permute-start.3 = (bf16[256,768]{0,1:T(8,128)(2,1)S(1)}, bf16[256,768]{0,1:T(8,128)(2,1)S(1)}, u32[]{:S(2)}, u32[]{:S(2)}) collective-permute-start(bf16[256,768]{0,1:T(8,128)(2,1)S(1)} %bitcast.92), channel_id=1, source_target_pairs={{0,8},{8,0},{1,9},{9,1},{2,10},{10,2},{3,11},{11,3},{4,12},{12,4},... | collective-permute-start | bytes 1179656 | tf_op jit(solution)/shard_map/ppermute | solution.py:17
  33.4 27.0 %copy-start.4 = (bf16[1,1,2,256,256]{4,3,2,1,0:T(8,128)(2,1)S(1)}, bf16[1,1,2,256,256]{4,3,2,1,0:T(8,128)(2,1)}, u32[]{:S(2)}) copy-start(bf16[1,1,2,256,256]{4,3,2,1,0:T(8,128)(2,1)} %param.9) | copy-start | bytes 786436
  63.8 2.8 %copy-start.2 = (bf16[2048,256]{1,0:T(8,128)(2,1)S(1)}, bf16[2048,256]{1,0:T(8,128)(2,1)}, u32[]{:S(2)}) copy-start(bf16[2048,256]{1,0:T(8,128)(2,1)} %param.11) | copy-start | bytes 3145732
where the time goes:
time: 69.5 us; the launch traced here: 69.3 us
  waiting for transfers between devices  32.9 us (47%)
  matrix products  13.5 us (19%)
  blocking collectives  11 us (16%)
  starting transfers between devices  7.99 us (11%)
  local copies, waits for them, and re-layouts  3.79 us (5%)
    ppermute x4, waiting for transfers between devices, from_partner(): return lax.ppermute(block, axis, route)  32.9 us
    all_gather x1, blocking collectives, shards(): lax.all_gather(coeffs[None], 'grp', axis=0, tiled=True)  11 us
    ppermute x4, starting transfers between devices, from_partner(): return lax.ppermute(block, axis, route)  7.99 us
    dot_general x2, matrix products, shards(): jnp.einsum('jckl,jlr->jckr', matrices, blocks, preferred_element_type=jnp...  5.88 us
    dot_general x1, matrix products, shards(): jnp.einsum('ctk,ckr->ctr', decoder_leaves, blocks, preferred_element_type...  2.68 us
    dot_general x1, matrix products, shards(): lax.dot_general(encoder, sources, (((0,), (0,)), ((), ())), preferred_ele...  2.23 us
    unnamed x10, local copies, waits for them, and re-layouts  1.9 us
    slice x2, local copies, waits for them, and re-layouts, shards(): local_weight[0, offset:offset + children].reshape(children // 2, 2, K, K)  1.88 us
  transfers between devices with their start and end apart: 4, of which 4 were waited for; matrix products, arithmetic and copies ran while one was open for 4% of the time, Pallas kernels for 0%

commit v1 on v0

--- a/solution.py
+++ b/solution.py
@@ -34,7 +34,9 @@
     merged = jnp.einsum(
         "hkl,hlr->kr",
         own_cross,
-        lax.all_gather(coeffs[None], "grp", axis=0, tiled=True),
+        jnp.concatenate(
+            lax.all_to_all(jnp.stack([coeffs[None]] * lax.axis_size("grp")), "grp", 0, 0), axis=0
+        ),
         preferred_element_type=jnp.float32,
     ).astype(jnp.bfloat16)
     blocks = merged[None]

time: 69.5 us -> 75.7 us (1.089)
  blocking collectives: 11 us -> 0 us
  waiting for transfers between devices: 32.9 us -> 41.3 us
  starting transfers between devices: 7.99 us -> 12.3 us
  local copies, waits for them, and re-layouts: 3.79 us -> 6.04 us
  matrix products: 13.5 us -> 14.7 us
  other arithmetic: 0 us -> 0.94 us
    all_gather x1 -> x0, blocking collectives: 11 us -> none  [shards(): lax.all_gather(coeffs[None], 'grp', axis=0, tiled=True)]
    all_to_all x0 -> x1, waiting for transfers between devices: none -> 6.47 us  [shards(): lax.all_to_all(jnp.stack([coeffs[None]] * lax.axis_size('grp')), 'grp', 0...]
    all_to_all x0 -> x1, starting transfers between devices: none -> 4.33 us  [shards(): lax.all_to_all(jnp.stack([coeffs[None]] * lax.axis_size('grp')), 'grp', 0...]
    slice x2, local copies, waits for them, and re-layouts: 1.88 us -> 4.14 us  [shards(): local_weight[0, offset:offset + children].reshape(children // 2, 2, K, K)]
    ppermute x4, waiting for transfers between devices: 32.9 us -> 34.8 us  [from_partner(): return lax.ppermute(block, axis, route)]
    dot_general x1, matrix products: 0.4 us -> 1.59 us  [shards(): jnp.einsum('hkl,hlr->kr', own_cross, jnp.concatenate(lax.all_to_all(jnp.s...]
    another operation x0 -> x1, other arithmetic: none -> 0.94 us  [shards(): jnp.stack([coeffs[None]] * lax.axis_size('grp'))]
    unnamed x10 -> x6, local copies, waits for them, and re-layouts: 1.9 us -> 1.89 us
  transfers between devices with their start and end apart: 4 -> 5, of which waited for: 4 -> 5; matrix products, arithmetic and copies ran while one was open for 4% -> 7% of each run, Pallas kernels for 0% -> 0%
where the time goes in v1:
time: 75.7 us; the launch traced here: 75.4 us
  waiting for transfers between devices  41.3 us (55%)
  matrix products  14.7 us (19%)
  starting transfers between devices  12.3 us (16%)
  local copies, waits for them, and re-layouts  6.04 us (8%)
  other arithmetic  0.94 us (1%)
    ppermute x4, waiting for transfers between devices, from_partner(): return lax.ppermute(block, axis, route)  34.8 us
    ppermute x4, starting transfers between devices, from_partner(): return lax.ppermute(block, axis, route)  7.98 us
    all_to_all x1, waiting for transfers between devices, shards(): lax.all_to_all(jnp.stack([coeffs[None]] * lax.axis_size('grp')), 'grp', 0...  6.47 us
    dot_general x2, matrix products, shards(): jnp.einsum('jckl,jlr->jckr', matrices, blocks, preferred_element_type=jnp...  5.88 us
    all_to_all x1, starting transfers between devices, shards(): lax.all_to_all(jnp.stack([coeffs[None]] * lax.axis_size('grp')), 'grp', 0...  4.33 us
    slice x2, local copies, waits for them, and re-layouts, shards(): local_weight[0, offset:offset + children].reshape(children // 2, 2, K, K)  4.14 us
    dot_general x1, matrix products, shards(): jnp.einsum('ctk,ckr->ctr', decoder_leaves, blocks, preferred_element_type...  2.68 us
    dot_general x1, matrix products, shards(): lax.dot_general(encoder, sources, (((0,), (0,)), ((), ())), preferred_ele...  2.23 us
  transfers between devices with their start and end apart: 5, of which 5 were waited for; matrix products, arithmetic and copies ran while one was open for 7% of the time, Pallas kernels for 0%

profile of v1, /device:TPU:0, one launch (start us, length us, event | category | flops | bytes accessed | tf_op | source)
XLA Modules:
  0.0 75.4 jit_solution(2160115678391193317)
XLA Ops:
  0.0 0.0 copy-start
  0.0 0.0 copy-start.2
  0.0 1.9 %copy-done = bf16[2048,768]{1,0:T(8,128)(2,1)S(1)} copy-done((bf16[2048,768]{1,0:T(8,128)(2,1)S(1)}, bf16[2048,768]{1,0:T(8,128)(2,1)}, u32[]{:S(2)}) %copy-start) | copy-done | bytes 3145752
  1.9 2.2 %convolution_convert_fusion.4 = bf16[256,768]{1,0:T(8,128)(2,1)S(1)} fusion(bf16[2048,256]{1,0:T(8,128)(2,1)} %param.7, bf16[2048,768]{1,0:T(8,128)(2,1)S(1)} %copy-done), kind=kOutput, calls=%fused_computation.15 | convolution fusion | flops 805502976 | bytes 4587520 | tf_op jit(solution)/shard_map/dot_general | solution.py:21
  4.1 0.6 collective-permute-start
  4.7 0.0 copy-done.2
  4.7 0.3 fusion.24
  5.0 1.0 %collective-permute-done = bf16[256,768]{1,0:T(8,128)(2,1)S(1)} collective-permute-done((bf16[256,768]{1,0:T(8,128)(2,1)S(1)}, bf16[256,768]{1,0:T(8,128)(2,1)S(1)}, u32[]{:S(2)}, u32[]{:S(2)}) %collective-permute-start) | collective-permute-done | bytes 393248 | tf_op jit(solution)/shard_map/ppermute | solution.py:17
  6.0 0.3 fusion.1
  6.4 2.9 %collective-permute-start.1 = (bf16[256,768]{0,1:T(8,128)(2,1)S(1)}, bf16[256,768]{0,1:T(8,128)(2,1)S(1)}, u32[]{:S(2)}, u32[]{:S(2)}) collective-permute-start(bf16[256,768]{0,1:T(8,128)(2,1)S(1)} %bitcast.93), channel_id=1, source_target_pairs={{0,2},{2,0},{1,3},{3,1},{4,6},{6,4},{5,7},{7,5},{8,10},{10,8},{9,1... | collective-permute-start | bytes 1179656 | tf_op jit(solution)/shard_map/ppermute | solution.py:17
  9.3 0.3 fusion.21
  9.6 9.1 %collective-permute-done.1 = bf16[256,768]{0,1:T(8,128)(2,1)S(1)} collective-permute-done((bf16[256,768]{0,1:T(8,128)(2,1)S(1)}, bf16[256,768]{0,1:T(8,128)(2,1)S(1)}, u32[]{:S(2)}, u32[]{:S(2)}) %collective-permute-start.1) | collective-permute-done | bytes 393248 | tf_op jit(solution)/shard_map/ppermute | solution.py:17
  18.7 0.3 fusion.2
  19.0 1.9 %collective-permute-start.2 = (bf16[256,768]{0,1:T(8,128)(2,1)S(1)}, bf16[256,768]{0,1:T(8,128)(2,1)S(1)}, u32[]{:S(2)}, u32[]{:S(2)}) collective-permute-start(bf16[256,768]{0,1:T(8,128)(2,1)S(1)} %bitcast.94), channel_id=1, source_target_pairs={{0,4},{4,0},{1,5},{5,1},{2,6},{6,2},{3,7},{7,3},{8,12},{12,8},{9,1... | collective-permute-start | bytes 1179656 | tf_op jit(solution)/shard_map/ppermute | solution.py:17
  20.9 0.3 fusion.18
  21.2 8.5 %collective-permute-done.2 = bf16[256,768]{0,1:T(8,128)(2,1)S(1)} collective-permute-done((bf16[256,768]{0,1:T(8,128)(2,1)S(1)}, bf16[256,768]{0,1:T(8,128)(2,1)S(1)}, u32[]{:S(2)}, u32[]{:S(2)}) %collective-permute-start.2) | collective-permute-done | bytes 393248 | tf_op jit(solution)/shard_map/ppermute | solution.py:17
  29.6 0.3 fusion.3
  29.9 2.6 %collective-permute-start.3 = (bf16[256,768]{0,1:T(8,128)(2,1)S(1)}, bf16[256,768]{0,1:T(8,128)(2,1)S(1)}, u32[]{:S(2)}, u32[]{:S(2)}) collective-permute-start(bf16[256,768]{0,1:T(8,128)(2,1)S(1)} %bitcast.95), channel_id=1, source_target_pairs={{0,8},{8,0},{1,9},{9,1},{2,10},{10,2},{3,11},{11,3},{4,12},{12,4},... | collective-permute-start | bytes 1179656 | tf_op jit(solution)/shard_map/ppermute | solution.py:17
  32.6 0.3 fusion.15
  32.8 16.2 %collective-permute-done.3 = bf16[256,768]{0,1:T(8,128)(2,1)S(1)} collective-permute-done((bf16[256,768]{0,1:T(8,128)(2,1)S(1)}, bf16[256,768]{0,1:T(8,128)(2,1)S(1)}, u32[]{:S(2)}, u32[]{:S(2)}) %collective-permute-start.3) | collective-permute-done | bytes 393248 | tf_op jit(solution)/shard_map/ppermute | solution.py:17
  49.0 0.3 fusion.6
  49.3 0.9 %pad_maximum_fusion = bf16[2,1,256,768]{2,3,1,0:T(8,128)(2,1)} fusion(bf16[1,1,256,768]{2,3,1,0:T(8,128)(2,1)S(1)} %fusion.6), kind=kLoop, calls=%fused_computation.18 | loop fusion | flops 393216 | bytes 1179648 | tf_op jit(solution)/shard_map/stack | solution.py:38
  50.3 4.3 %all-to-all-start = ((bf16[2,1,256,768]{2,3,1,0:T(8,128)(2,1)}), bf16[2,1,256,768]{2,3,1,0:T(8,128)(2,1)}, u32[]{:S(2)}, u32[]{:S(2)}) async-start(bf16[2,1,256,768]{2,3,1,0:T(8,128)(2,1)} %pad_maximum_fusion), calls=%async_computation | async-start | bytes 1572864 | tf_op jit(solution)/shard_map/all_to_all | solution.py:38
  54.6 1.9 %slice.42 = bf16[1,4,256,256]{3,2,1,0:T(8,128)(2,1)} slice(bf16[1,14,256,256]{3,2,1,0:T(8,128)(2,1)} %param.10), slice={[0:1], [2:6], [0:256], [0:256]} | slice | bytes 1048576 | tf_op jit(solution)/shard_map/slice | solution.py:46
  56.5 2.3 %slice.43 = bf16[1,8,256,256]{3,2,1,0:T(8,128)(2,1)} slice(bf16[1,14,256,256]{3,2,1,0:T(8,128)(2,1)} %param.10), slice={[0:1], [6:14], [0:256], [0:256]} | slice | bytes 2097152 | tf_op jit(solution)/shard_map/slice | solution.py:46
  58.7 6.5 %all-to-all-done = bf16[2,1,256,768]{2,3,1,0:T(8,128)(2,1)} async-done(((bf16[2,1,256,768]{2,3,1,0:T(8,128)(2,1)}), bf16[2,1,256,768]{2,3,1,0:T(8,128)(2,1)}, u32[]{:S(2)}, u32[]{:S(2)}) %all-to-all-start) | async-done | bytes 786464 | tf_op jit(solution)/shard_map/all_to_all | solution.py:38
  65.2 1.6 %fusion.7 = bf16[768,256,1]{1,0,2:T(8,128)(2,1)S(1)} fusion(bf16[2,1,256,768]{2,3,1,0:T(8,128)(2,1)} %all-to-all-done, bf16[1,1,2,256,256]{4,3,2,1,0:T(8,128)(2,1)} %param.9), kind=kOutput, calls=%fused_computation.17 | convolution fusion | flops 201523200 | bytes 1441792 | tf_op jit(solution)/shard_map/hkl,hlr->kr/dot_general | solution.py:34
  66.8 3.1 %convolution_convert_fusion.2 = bf16[2,768,2,256]{3,1,2,0:T(8,128)(2,1)} fusion(bf16[2,2,256,256]{3,2,1,0:T(8,128)(2,1)} %bitcast.92, bf16[768,256,1]{1,0,2:T(8,128)(2,1)S(1)} %fusion.7, bf16[1,14,256,256]{3,2,1,0:T(8,128)(2,1)} %param.10), kind=kOutput, calls=%fused_computation.2 | convolution fusion | flops 605159424 | bytes 2752512 | tf_op jit(solution)/shard_map/jckl,jlr->jckr/dot_general | solution.py:47
  69.9 0.0 copy-start.1
  69.9 2.8 %convolution_convert_fusion.1 = bf16[4,768,2,256]{3,1,2,0:T(8,128)(2,1)S(1)} fusion(bf16[4,256,768,1]{1,2,3,0:T(8,128)(2,1)} %bitcast.90, bf16[4,2,256,256]{3,2,1,0:T(8,128)(2,1)} %bitcast.91), kind=kOutput, calls=%fused_computation.1 | convolution fusion | flops 806879232 | bytes 5767168 | tf_op jit(solution)/shard_map/jckl,jlr->jckr/dot_general | solution.py:47
  72.7 0.0 copy-done.1
  72.7 2.7 %convolution_convert_fusion = bf16[8,768,256]{1,2,0:T(8,128)(2,1)} fusion(bf16[8,256,768]{1,2,0:T(8,128)(2,1)S(1)} %bitcast.89, bf16[8,256,256]{2,1,0:T(8,128)(2,1)S(1)} %bitcast.96), kind=kOutput, calls=%fused_computation | convolution fusion | flops 806879232 | bytes 7340032 | tf_op jit(solution)/shard_map/ctk,ckr->ctr/dot_general | solution.py:51
Async XLA Ops:
  0.0 1.9 %copy-start = (bf16[2048,768]{1,0:T(8,128)(2,1)S(1)}, bf16[2048,768]{1,0:T(8,128)(2,1)}, u32[]{:S(2)}) copy-start(bf16[2048,768]{1,0:T(8,128)(2,1)} %param.6) | copy-start | bytes 9437188
  0.0 4.7 %copy-start.2 = (bf16[1,4,2,256,256]{4,3,2,1,0:T(8,128)(2,1)S(1)}, bf16[1,4,2,256,256]{4,3,2,1,0:T(8,128)(2,1)}, u32[]{:S(2)}) copy-start(bf16[1,4,2,256,256]{4,3,2,1,0:T(8,128)(2,1)} %param.8) | copy-start | bytes 3145732
  4.1 1.9 %collective-permute-start = (bf16[256,768]{1,0:T(8,128)(2,1)S(1)}, bf16[256,768]{1,0:T(8,128)(2,1)S(1)}, u32[]{:S(2)}, u32[]{:S(2)}) collective-permute-start(bf16[256,768]{1,0:T(8,128)(2,1)S(1)} %convolution_convert_fusion.4), channel_id=1, source_target_pairs={{0,1},{1,0},{2,3},{3,2},{4,5},{5,4},{6,7},{7,6},{8,9},{9,8},{10,11... | collective-permute-start | bytes 1179656 | tf_op jit(solution)/shard_map/ppermute | solution.py:17
  6.4 12.3 %collective-permute-start.1 = (bf16[256,768]{0,1:T(8,128)(2,1)S(1)}, bf16[256,768]{0,1:T(8,128)(2,1)S(1)}, u32[]{:S(2)}, u32[]{:S(2)}) collective-permute-start(bf16[256,768]{0,1:T(8,128)(2,1)S(1)} %bitcast.93), channel_id=1, source_target_pairs={{0,2},{2,0},{1,3},{3,1},{4,6},{6,4},{5,7},{7,5},{8,10},{10,8},{9,1... | collective-permute-start | bytes 1179656 | tf_op jit(solution)/shard_map/ppermute | solution.py:17
  19.0 10.6 %collective-permute-start.2 = (bf16[256,768]{0,1:T(8,128)(2,1)S(1)}, bf16[256,768]{0,1:T(8,128)(2,1)S(1)}, u32[]{:S(2)}, u32[]{:S(2)}) collective-permute-start(bf16[256,768]{0,1:T(8,128)(2,1)S(1)} %bitcast.94), channel_id=1, source_target_pairs={{0,4},{4,0},{1,5},{5,1},{2,6},{6,2},{3,7},{7,3},{8,12},{12,8},{9,1... | collective-permute-start | bytes 1179656 | tf_op jit(solution)/shard_map/ppermute | solution.py:17
  29.9 19.1 %collective-permute-start.3 = (bf16[256,768]{0,1:T(8,128)(2,1)S(1)}, bf16[256,768]{0,1:T(8,128)(2,1)S(1)}, u32[]{:S(2)}, u32[]{:S(2)}) collective-permute-start(bf16[256,768]{0,1:T(8,128)(2,1)S(1)} %bitcast.95), channel_id=1, source_target_pairs={{0,8},{8,0},{1,9},{9,1},{2,10},{10,2},{3,11},{11,3},{4,12},{12,4},... | collective-permute-start | bytes 1179656 | tf_op jit(solution)/shard_map/ppermute | solution.py:17
  50.3 14.9 %all-to-all-start = ((bf16[2,1,256,768]{2,3,1,0:T(8,128)(2,1)}), bf16[2,1,256,768]{2,3,1,0:T(8,128)(2,1)}, u32[]{:S(2)}, u32[]{:S(2)}) async-start(bf16[2,1,256,768]{2,3,1,0:T(8,128)(2,1)} %pad_maximum_fusion), calls=%async_computation | async-start | bytes 1572864 | tf_op jit(solution)/shard_map/all_to_all | solution.py:38
  69.9 2.8 %copy-start.1 = (bf16[2048,256]{1,0:T(8,128)(2,1)S(1)}, bf16[2048,256]{1,0:T(8,128)(2,1)}, u32[]{:S(2)}) copy-start(bf16[2048,256]{1,0:T(8,128)(2,1)} %param.11) | copy-start | bytes 3145732
